TPU v7x, 512 devices: a whole 4x8x8 slice. The times are simulated.
512 devices in a mesh: ab: 16 (over y, x_lo), cd: 32 (over z, x_hi, core).
Axes of the slice: x: 4 (x_hi: 2, x_lo: 2; x = x_hi * 2 + x_lo), y: 8, z: 8, core: 2. Of those that a mesh axis runs over, the one named last changes fastest.
Arguments:
- factors: bfloat16 [128, 128, 2048], P('ab', 'cd'), may hold values from -0.25 to 0.25
- amplitudes: float32 [256, 128, 128], P('cd', 'ab'), may hold values from -4 to 4
- driving: float32 [256, 128, 128], P('cd', 'ab'), may hold values from -8 to 8
- occ_energy: float32 [32], replicated, may hold values from -2 to -0.5
- vir_energy: float32 [128], replicated, may hold values from 0.5 to 3
Outputs:
- new_amplitudes: float32 [256, 128, 128], P('cd', 'ab')
- residual: float32 [256, 128, 128], P('cd', 'ab')
All inputs are finite; a program needn't handle non-finite values.
Results may differ from a plain program's by a relative error of at most 0.0036.
Values may be sent and summed in bfloat16 or wider, within the bound.
No kernel may reach another device: no remote copies, remote signals or barrier semaphores. Data moves between devices by JAX's collectives and lax.ppermute only.
A program may use at most 64 MiB of HBM per device.

v0:
```python
import jax
import jax.numpy as jnp
from jax import lax
from jax.sharding import PartitionSpec as P

ITERS = 2


def local(factors, amplitudes, driving, occ_energy, vir_energy):
    rows = amplitudes.shape[0]
    a_local = amplitudes.shape[1]
    virtuals = amplitudes.shape[2]
    aux_width = factors.shape[2]
    n_cd = lax.axis_size("cd")
    d_local = factors.shape[1]
    pairs = rows * n_cd
    cd_index = lax.axis_index("cd")
    ab_index = lax.axis_index("ab")
    left_rows = lax.all_gather(factors, "cd", axis=1, tiled=True)
    left_flat = left_rows.reshape(a_local * virtuals, aux_width)
    piece = lax.all_gather(factors, "ab", axis=0, tiled=True)
    count = piece.shape[0]
    product = lax.dot_general(
        left_flat,
        piece.reshape(count * d_local, aux_width),
        (((1,), (1,)), ((), ())),
        preferred_element_type=jnp.float32,
    )
    product = product.reshape(a_local, virtuals, count, d_local)
    tiles = (
        product.transpose(0, 2, 3, 1)
        .reshape(a_local, count, d_local * virtuals)
        .astype(jnp.bfloat16)
    )
    tiles = tiles.reshape(a_local * virtuals, d_local * virtuals)
    n_occ = occ_energy.shape[0]
    row_ids = cd_index * rows + lax.iota(jnp.int32, rows)
    orbitals = lax.iota(jnp.int32, n_occ)
    first_hot = (row_ids[:, None] // n_occ == orbitals[None, :]).astype(jnp.float32)
    second_hot = (row_ids[:, None] % n_occ == orbitals[None, :]).astype(jnp.float32)
    occ_pair = jnp.sum((first_hot + second_hot) * occ_energy[None, :], axis=1)
    vir_rows = lax.dynamic_slice_in_dim(vir_energy, ab_index * a_local, a_local)
    denominator = vir_rows[None, :, None] + vir_energy[None, None, :] - occ_pair[:, None, None]
    current = amplitudes
    residual = amplitudes
    for step in range(ITERS):
        rounded = current.astype(jnp.bfloat16)
        every_row = lax.all_gather(rounded, "cd", axis=0, tiled=True)
        columns = lax.dynamic_slice_in_dim(every_row, cd_index * d_local, d_local, 2)
        own_block = columns.transpose(2, 1, 0)
        gathered = lax.all_gather(own_block, "ab", axis=1, tiled=True)
        flat_amps = gathered.reshape(d_local * virtuals, pairs)
        summed = lax.psum_scatter(
            lax.dot_general(
                flat_amps, tiles, (((0,), (1,)), ((), ())), preferred_element_type=jnp.float32
            ),
            "cd",
            scatter_dimension=0,
            tiled=True,
        ).reshape(rows, a_local, virtuals)
        mirrored = lax.all_to_all(summed, "ab", split_axis=2, concat_axis=1, tiled=True).transpose(
            0, 2, 1
        )
        symmetric = 0.5 * (summed + mirrored)
        residual = driving + denominator * current + symmetric
        current = current - residual / denominator
    return (current, residual)


def solution(mesh):
    placed = (P("ab", "cd", None), P("cd", "ab", None), P("cd", "ab", None), P(), P())
    return jax.shard_map(
        local,
        mesh=mesh,
        in_specs=placed,
        out_specs=(P("cd", "ab", None), P("cd", "ab", None)),
        check_vma=False,
    )
```

profile of v0, /device:TPU:4, one launch (start us, length us, event | category | flops | bytes accessed | tf_op | source)
XLA Modules:
  0.0 559.9 jit_solution(14078645966678964496)
XLA Ops:
  7.2 0.0 all-gather.5.cloned.1.call-start
  7.2 1.6 copy.37
  8.8 0.0 all-gather.5.cloned.1.call-update
  8.9 0.0 all-gather.3.cloned.1.call-start
  8.9 0.7 all-gather.3.cloned.1.call-update
  9.6 0.0 reduce-scatter.3.cloned.1.call-start
  9.7 0.8 convert_element_type.25
  10.4 45.7 %all_gather.18 = bf16[256,8,128]{2,1,0:T(8,128)(2,1)S(1)} all-gather(bf16[8,8,128]{2,1,0:T(8,128)(2,1)S(1)} %convert_element_type.25), channel_id=1, replica_groups=mesh['ab'=16,'cd'=32] {'cd'}, dimensions={0}, use_global_device_ids=true | all-gather | bytes 540672 | tf_op jit(solution)/shard_map/all_gather | solution.py:48
  56.1 0.2 constant_dynamic-slice_fusion.1
  56.3 0.3 copy.57
  56.7 36.1 %all_gather.19 = bf16[4,128,256]{2,1,0:T(8,128)(2,1)S(1)} all-gather(bf16[4,8,256]{2,1,0:T(8,128)(2,1)S(1)} %bitcast.73), channel_id=1, replica_groups=mesh['ab'=16,'cd'=32] {'ab'}, dimensions={1}, use_global_device_ids=true | all-gather | bytes 278528 | tf_op jit(solution)/shard_map/all_gather | solution.py:51
  92.8 0.0 all-gather.5.cloned.1.call-done
  92.8 92.8 %all-gather.3.cloned.1.call-done = bf16[8,128,2048]{2,0,1:T(8,128)(2,1)} async-done(((bf16[8,4,2048]{2,0,1:T(8,128)(2,1)}), bf16[8,128,2048]{2,0,1:T(8,128)(2,1)}) %all-gather.3.cloned.1.call-update) | async-done | bytes 4194320 | tf_op jit(solution)/shard_map/all_gather | solution.py:19
  185.5 7.7 %fusion.8 = bf16[8,128,4,128]{1,3,2,0:T(8,128)(2,1)S(1)} fusion(bf16[128,4,2048]{2,0,1:T(8,128)(2,1)} %all-gather.5.cloned.1.call-done, bf16[8,128,2048,1]{2,0,1,3:T(8,128)(2,1)} %bitcast.75), kind=kOutput, calls=%fused_computation.4 | convolution fusion | flops 2148007936 | bytes 7340032 | tf_op jit(solution)/shard_map/dot_general | solution.py:23
  193.2 0.0 copy-start.2
  193.2 0.0 copy-start.3
  193.2 0.0 copy-start
  193.2 0.0 copy-start.1
  193.2 0.7 copy.40
  193.9 1.4 fusion.15
  195.4 0.0 reduce-scatter.3.cloned.1.call-update
  195.4 0.0 copy-done.2
  195.4 0.1 dynamic_slice.9
  195.5 0.1 broadcast_add_fusion
  195.6 122.6 %reduce-scatter.3.cloned.1.call-done = f32[8,1024]{1,0:T(8,128)} async-done(((f32[256,1024]{1,0:T(8,128)}), f32[8,1024]{1,0:T(8,128)}) %reduce-scatter.3.cloned.1.call-update) | async-done | bytes 32784 | tf_op jit(solution)/shard_map/reduce_scatter | solution.py:53
  318.1 1.0 copy.41
  319.1 0.9 reshape.124
  320.0 7.4 %all-to-all-start = ((f32[16,1,512]{2,1,0:T(1,128)}), f32[16,1,512]{2,1,0:T(1,128)S(1)}, u32[]{:S(2)}, u32[]{:S(2)}) async-start(f32[16,1,512]{2,1,0:T(1,128)} %reshape.124), calls=%async_computation.1 | async-start | bytes 65536 | tf_op jit(solution)/shard_map/all_to_all | solution.py:61
  327.4 0.0 reduce-scatter.5.cloned.1.call-start
  327.4 0.0 copy-done.3
  327.5 0.2 multiply_reduce_fusion
  327.6 8.5 %all-to-all-done = f32[16,1,512]{2,1,0:T(1,128)S(1)} async-done(((f32[16,1,512]{2,1,0:T(1,128)}), f32[16,1,512]{2,1,0:T(1,128)S(1)}, u32[]{:S(2)}, u32[]{:S(2)}) %all-to-all-start) | async-done | bytes 32800 | tf_op jit(solution)/shard_map/all_to_all | solution.py:61
  336.2 0.5 broadcast.123
  336.7 0.7 reduce
  337.4 0.3 reshape.125
  337.7 0.3 copy.43
  338.0 0.3 all_to_all.29
  338.3 0.0 copy-done
  338.3 0.0 copy-done.1
  338.3 0.8 fusion.28
  339.2 38.9 %all_gather.22 = bf16[256,8,128]{2,1,0:T(8,128)(2,1)S(1)} all-gather(bf16[8,8,128]{2,1,0:T(8,128)(2,1)S(1)} %get-tuple-element.4), channel_id=1, replica_groups=mesh['ab'=16,'cd'=32] {'cd'}, dimensions={0}, use_global_device_ids=true | all-gather | bytes 540672 | tf_op jit(solution)/shard_map/all_gather | solution.py:48
  378.0 0.2 constant_dynamic-slice_fusion
  378.2 0.4 copy.58
  378.6 32.1 %all_gather.23 = bf16[4,128,256]{2,1,0:T(8,128)(2,1)S(1)} all-gather(bf16[4,8,256]{2,1,0:T(8,128)(2,1)S(1)} %bitcast.74), channel_id=1, replica_groups=mesh['ab'=16,'cd'=32] {'ab'}, dimensions={1}, use_global_device_ids=true | all-gather | bytes 278528 | tf_op jit(solution)/shard_map/all_gather | solution.py:51
  410.7 1.4 fusion.13
  412.1 0.0 reduce-scatter.5.cloned.1.call-update
  412.1 120.8 %reduce-scatter.5.cloned.1.call-done = f32[8,1024]{1,0:T(8,128)} async-done(((f32[256,1024]{1,0:T(8,128)}), f32[8,1024]{1,0:T(8,128)}) %reduce-scatter.5.cloned.1.call-update) | async-done | bytes 32784 | tf_op jit(solution)/shard_map/reduce_scatter | solution.py:53
  532.9 1.0 copy.46
  533.9 0.3 reshape.126
  534.2 16.0 %all_to_all.36 = f32[16,1,512]{2,1,0:T(1,128)S(1)} all-to-all(f32[16,1,512]{2,1,0:T(1,128)S(1)} %reshape.126), channel_id=1, replica_groups=mesh['ab'=16,'cd'=32] {'ab'}, dimensions={0} | all-to-all | bytes 65536 | tf_op jit(solution)/shard_map/all_to_all | solution.py:61
  550.3 0.7 reduce.1
  551.0 0.3 reshape.127
  551.3 0.3 copy.48
  551.6 0.3 all_to_all.33
  551.9 1.5 fusion.24
  (1 shorter events, 0.0 us)
Async XLA Ops:
  7.2 85.6 %all-gather.5.cloned.1.call-start = ((), (), s32[]{:S(2)}) async-start(), calls=%async_computation.5 | async-start | bytes 2228224 | tf_op jit(solution)/shard_map/all_gather | solution.py:21
  8.9 176.7 %all-gather.3.cloned.1.call-start = ((), (), s32[]{:S(2)}) async-start(), calls=%async_computation.4 | async-start | bytes 4325376 | tf_op jit(solution)/shard_map/all_gather | solution.py:19
  9.6 308.5 %reduce-scatter.3.cloned.1.call-start = ((), (), s32[]{:S(2)}) async-start(), calls=%async_computation.6 | async-start | bytes 1081344 | tf_op jit(solution)/shard_map/reduce_scatter | solution.py:53
  193.2 2.2 copy-start.2
  193.2 134.2 %copy-start.3 = (f32[32]{0:T(128)S(1)}, f32[32]{0:T(128)}, u32[]{:S(2)}) copy-start(f32[32]{0:T(128)} %param.8) | copy-start | bytes 388
  193.2 145.1 %copy-start = (f32[8,8,128]{2,1,0:T(8,128)S(1)}, f32[8,8,128]{2,1,0:T(8,128)}, u32[]{:S(2)}) copy-start(f32[8,8,128]{2,1,0:T(8,128)} %param.7) | copy-start | bytes 98308
  193.2 145.1 %copy-start.1 = (f32[8,8,128]{2,1,0:T(8,128)S(1)}, f32[8,8,128]{2,1,0:T(8,128)}, u32[]{:S(2)}) copy-start(f32[8,8,128]{2,1,0:T(8,128)} %param.6) | copy-start | bytes 98308
  320.0 16.1 %all-to-all-start = ((f32[16,1,512]{2,1,0:T(1,128)}), f32[16,1,512]{2,1,0:T(1,128)S(1)}, u32[]{:S(2)}, u32[]{:S(2)}) async-start(f32[16,1,512]{2,1,0:T(1,128)} %reshape.124), calls=%async_computation.1 | async-start | bytes 65536 | tf_op jit(solution)/shard_map/all_to_all | solution.py:61
  327.4 205.5 %reduce-scatter.5.cloned.1.call-start = ((), (), s32[]{:S(2)}) async-start(), calls=%async_computation.7 | async-start | bytes 1081344 | tf_op jit(solution)/shard_map/reduce_scatter | solution.py:53
Sparse Core Ops, SparseCore 0:
  10.1 82.6 all-gather.4
  96.1 89.3 all-gather.2
  195.5 122.5 reduce-scatter.2
  412.2 120.6 reduce-scatter.4
where the time goes:
time: 560 us
  waiting for transfers between devices  345 us (62%)
  blocking collectives  169 us (30%)
  between operations  13.9 us (2%)
  matrix products  10.5 us (2%)
  local copies, waits for them, and re-layouts  8.95 us (2%)
  starting transfers between devices  7.52 us (1%)
    reduce_scatter x2, waiting for transfers between devices, local(): lax.psum_scatter(lax.dot_general(flat_amps, tiles, (((0,), (1,)), ((), ()...  243 us
    all_gather x1, waiting for transfers between devices, local(): left_rows = lax.all_gather(factors, 'cd', axis=1, tiled=True)  92.8 us
    all_gather x2, blocking collectives, local(): every_row = lax.all_gather(rounded, 'cd', axis=0, tiled=True)  84.5 us
    all_gather x2, blocking collectives, local(): gathered = lax.all_gather(own_block, 'ab', axis=1, tiled=True)  68.2 us
    all_to_all x1, blocking collectives, local(): lax.all_to_all(summed, 'ab', split_axis=2, concat_axis=1, tiled=True)  16 us
  transfers between devices with their start and end apart: 5, of which 4 were waited for; matrix products, arithmetic and copies ran while one was open for 0% of the time, Pallas kernels for 0%

commit v1 on v0

--- a/solution.py
+++ b/solution.py
@@ -16,7 +16,9 @@
     pairs = rows * n_cd
     cd_index = lax.axis_index("cd")
     ab_index = lax.axis_index("ab")
-    left_rows = lax.all_gather(factors, "cd", axis=1, tiled=True)
+    left_rows = jnp.concatenate(
+        lax.all_to_all(jnp.stack([factors] * lax.axis_size("cd")), "cd", 0, 0), axis=1
+    )
     left_flat = left_rows.reshape(a_local * virtuals, aux_width)
     piece = lax.all_gather(factors, "ab", axis=0, tiled=True)
     count = piece.shape[0]

time: 560 us -> 572 us (1.021)
  waiting for transfers between devices: 345 us -> 250 us
  blocking collectives: 169 us -> 247 us
  local copies, waits for them, and re-layouts: 8.95 us -> 27 us
  starting transfers between devices: 7.52 us -> 21.3 us
    all_gather x1 -> x0, waiting for transfers between devices: 92.8 us -> none  [local(): left_rows = lax.all_gather(factors, 'cd', axis=1, tiled=True)]
    all_gather x2, blocking collectives: 84.5 us -> 164 us  [local(): every_row = lax.all_gather(rounded, 'cd', axis=0, tiled=True)]
    all_to_all x0 -> x1, starting transfers between devices: none -> 13.6 us  [local(): lax.all_to_all(jnp.stack([factors] * lax.axis_size('cd')), 'cd', 0, 0)]
    reshape x0 -> x1, local copies, waits for them, and re-layouts: none -> 7.07 us  [local(): jnp.concatenate(lax.all_to_all(jnp.stack([factors] * lax.axis_size('cd'))...]
    dot_general x0 -> x1, local copies, waits for them, and re-layouts: none -> 6.88 us  [local(): lax.dot_general(left_flat, piece.reshape(count * d_local, aux_width), (((...]
  transfers between devices with their start and end apart: 5 -> 5, of which waited for: 4 -> 3; matrix products, arithmetic and copies ran while one was open for 0% -> 3% of each run, Pallas kernels for 0% -> 0%
where the time goes in v1:
time: 572 us
  waiting for transfers between devices  250 us (44%)
  blocking collectives  247 us (43%)
  local copies, waits for them, and re-layouts  27 us (5%)
  starting transfers between devices  21.3 us (4%)
  between operations  13.9 us (2%)
  matrix products  8.11 us (1%)
    reduce_scatter x2, waiting for transfers between devices, local(): lax.psum_scatter(lax.dot_general(flat_amps, tiles, (((0,), (1,)), ((), ()...  242 us
    all_gather x2, blocking collectives, local(): every_row = lax.all_gather(rounded, 'cd', axis=0, tiled=True)  164 us
    all_gather x2, blocking collectives, local(): gathered = lax.all_gather(own_block, 'ab', axis=1, tiled=True)  67.1 us
    all_to_all x1, blocking collectives, local(): lax.all_to_all(summed, 'ab', split_axis=2, concat_axis=1, tiled=True)  16 us
    all_to_all x1, starting transfers between devices, local(): lax.all_to_all(jnp.stack([factors] * lax.axis_size('cd')), 'cd', 0, 0)  13.6 us
  transfers between devices with their start and end apart: 5, of which 3 were waited for; matrix products, arithmetic and copies ran while one was open for 3% of the time, Pallas kernels for 0%

profile of v1, /device:TPU:4, one launch (start us, length us, event | category | flops | bytes accessed | tf_op | source)
XLA Modules:
  0.0 571.6 jit_solution(13106134802997649244)
XLA Ops:
  7.2 5.0 stack.2
  12.2 0.0 copy-start
  12.2 0.0 copy-start.2
  12.2 13.6 %all-to-all-start = ((bf16[32,8,4,2048]{3,2,1,0:T(4,128)(2,1)}), bf16[32,8,4,2048]{3,2,1,0:T(4,128)(2,1)}, u32[]{:S(2)}, u32[]{:S(2)}) async-start(bf16[32,8,4,2048]{3,2,1,0:T(4,128)(2,1)} %stack.2), calls=%async_computation | async-start | bytes 8388608 | tf_op jit(solution)/shard_map/all_to_all | solution.py:20
  25.8 0.0 all-gather.2.cloned.1.call-start
  25.9 0.0 copy-done
  25.9 0.7 copy.37
  26.6 0.0 all-gather.2.cloned.1.call-update
  26.6 0.0 reduce-scatter.3.cloned.1.call-start
  26.7 0.0 copy-done.2
  26.7 125.4 %all_gather.15 = bf16[256,8,128]{2,1,0:T(8,128)(2,1)S(1)} all-gather(bf16[8,8,128]{2,1,0:T(8,128)(2,1)S(1)} %convert_element_type.25), channel_id=1, replica_groups=mesh['ab'=16,'cd'=32] {'cd'}, dimensions={0}, use_global_device_ids=true | all-gather | bytes 540672 | tf_op jit(solution)/shard_map/all_gather | solution.py:50
  152.1 0.2 constant_dynamic-slice_fusion.1
  152.3 0.3 copy.53
  152.6 35.0 %all_gather.16 = bf16[4,128,256]{2,1,0:T(8,128)(2,1)S(1)} all-gather(bf16[4,8,256]{2,1,0:T(8,128)(2,1)S(1)} %bitcast.80), channel_id=1, replica_groups=mesh['ab'=16,'cd'=32] {'ab'}, dimensions={1}, use_global_device_ids=true | all-gather | bytes 278528 | tf_op jit(solution)/shard_map/all_gather | solution.py:53
  187.7 0.0 all-to-all-done
  187.7 7.1 %copy.36 = bf16[8,32,4,2048]{3,2,1,0:T(4,128)(2,1)} copy(bf16[8,32,4,2048]{3,2,0,1:T(4,128)(2,1)} %bitcast.2) | data formatting | bytes 8388608 | tf_op jit(solution)/shard_map/reshape | solution.py:19
  194.7 6.9 %reshape.127 = bf16[8,128,2048,1]{2,1,0,3:T(8,128)(2,1)} reshape(bf16[8,32,4,2048]{3,2,1,0:T(4,128)(2,1)} %copy.36) | data formatting | bytes 8388608 | tf_op jit(solution)/shard_map/dot_general | solution.py:25
  201.6 0.0 all-gather.2.cloned.1.call-done
  201.6 5.2 fusion.8
  206.8 0.0 copy-start.3
  206.8 0.0 copy-start.4
  206.9 0.0 copy-start.1
  206.9 0.7 copy.38
  207.6 1.4 fusion.15
  209.0 0.0 reduce-scatter.3.cloned.1.call-update
  209.0 0.0 copy-done.3
  209.1 0.1 dynamic_slice.9
  209.1 0.1 broadcast_add_fusion
  209.2 120.6 %reduce-scatter.3.cloned.1.call-done = f32[8,1024]{1,0:T(8,128)} async-done(((f32[256,1024]{1,0:T(8,128)}), f32[8,1024]{1,0:T(8,128)}) %reduce-scatter.3.cloned.1.call-update) | async-done | bytes 32784 | tf_op jit(solution)/shard_map/reduce_scatter | solution.py:55
  329.8 1.0 copy.39
  330.8 0.9 reshape.130
  331.7 7.5 %all-to-all-start.1 = ((f32[16,1,512]{2,1,0:T(1,128)}), f32[16,1,512]{2,1,0:T(1,128)S(1)}, u32[]{:S(2)}, u32[]{:S(2)}) async-start(f32[16,1,512]{2,1,0:T(1,128)} %reshape.130), calls=%async_computation.2 | async-start | bytes 65536 | tf_op jit(solution)/shard_map/all_to_all | solution.py:63
  339.3 0.0 reduce-scatter.5.cloned.1.call-start
  339.3 0.0 copy-done.4
  339.3 0.2 multiply_reduce_fusion
  339.5 8.5 %all-to-all-done.1 = f32[16,1,512]{2,1,0:T(1,128)S(1)} async-done(((f32[16,1,512]{2,1,0:T(1,128)}), f32[16,1,512]{2,1,0:T(1,128)S(1)}, u32[]{:S(2)}, u32[]{:S(2)}) %all-to-all-start.1) | async-done | bytes 32800 | tf_op jit(solution)/shard_map/all_to_all | solution.py:63
  348.1 0.5 broadcast.125
  348.6 0.7 reduce
  349.3 0.3 reshape.131
  349.6 0.3 copy.41
  349.9 0.3 all_to_all.33
  350.2 0.0 copy-done.1
  350.2 0.8 fusion.28
  351.0 38.7 %all_gather.18 = bf16[256,8,128]{2,1,0:T(8,128)(2,1)S(1)} all-gather(bf16[8,8,128]{2,1,0:T(8,128)(2,1)S(1)} %get-tuple-element.4), channel_id=1, replica_groups=mesh['ab'=16,'cd'=32] {'cd'}, dimensions={0}, use_global_device_ids=true | all-gather | bytes 540672 | tf_op jit(solution)/shard_map/all_gather | solution.py:50
  389.7 0.2 constant_dynamic-slice_fusion
  389.9 0.4 copy.54
  390.3 32.1 %all_gather.19 = bf16[4,128,256]{2,1,0:T(8,128)(2,1)S(1)} all-gather(bf16[4,8,256]{2,1,0:T(8,128)(2,1)S(1)} %bitcast.81), channel_id=1, replica_groups=mesh['ab'=16,'cd'=32] {'ab'}, dimensions={1}, use_global_device_ids=true | all-gather | bytes 278528 | tf_op jit(solution)/shard_map/all_gather | solution.py:53
  422.4 1.4 fusion.13
  423.8 0.0 reduce-scatter.5.cloned.1.call-update
  423.8 120.9 %reduce-scatter.5.cloned.1.call-done = f32[8,1024]{1,0:T(8,128)} async-done(((f32[256,1024]{1,0:T(8,128)}), f32[8,1024]{1,0:T(8,128)}) %reduce-scatter.5.cloned.1.call-update) | async-done | bytes 32784 | tf_op jit(solution)/shard_map/reduce_scatter | solution.py:55
  544.7 1.0 copy.44
  545.7 0.3 reshape.132
  546.0 16.0 %all_to_all.41 = f32[16,1,512]{2,1,0:T(1,128)S(1)} all-to-all(f32[16,1,512]{2,1,0:T(1,128)S(1)} %reshape.132), channel_id=1, replica_groups=mesh['ab'=16,'cd'=32] {'ab'}, dimensions={0} | all-to-all | bytes 65536 | tf_op jit(solution)/shard_map/all_to_all | solution.py:63
  562.0 0.7 reduce.1
  562.8 0.3 reshape.133
  563.1 0.3 copy.46
  563.4 0.3 all_to_all.37
  563.6 1.5 fusion.24
  (2 shorter events, 0.0 us)
Async XLA Ops:
  12.2 13.7 %copy-start = (bf16[8,4,2048]{2,1,0:T(4,128)(2,1)S(1)}, bf16[8,4,2048]{2,1,0:T(4,128)(2,1)}, u32[]{:S(2)}) copy-start(bf16[8,4,2048]{2,1,0:T(4,128)(2,1)} %param.5) | copy-start | bytes 393220
  12.2 14.5 %copy-start.2 = (f32[8,8,128]{2,1,0:T(8,128)S(1)}, f32[8,8,128]{2,1,0:T(8,128)}, u32[]{:S(2)}) copy-start(f32[8,8,128]{2,1,0:T(8,128)} %param.6) | copy-start | bytes 98308
  12.2 175.5 %all-to-all-start = ((bf16[32,8,4,2048]{3,2,1,0:T(4,128)(2,1)}), bf16[32,8,4,2048]{3,2,1,0:T(4,128)(2,1)}, u32[]{:S(2)}, u32[]{:S(2)}) async-start(bf16[32,8,4,2048]{3,2,1,0:T(4,128)(2,1)} %stack.2), calls=%async_computation | async-start | bytes 8388608 | tf_op jit(solution)/shard_map/all_to_all | solution.py:20
  25.8 175.8 %all-gather.2.cloned.1.call-start = ((), (), s32[]{:S(2)}) async-start(), calls=%async_computation.5 | async-start | bytes 2228224 | tf_op jit(solution)/shard_map/all_gather | solution.py:23
  26.6 303.2 %reduce-scatter.3.cloned.1.call-start = ((), (), s32[]{:S(2)}) async-start(), calls=%async_computation.6 | async-start | bytes 1081344 | tf_op jit(solution)/shard_map/reduce_scatter | solution.py:55
  206.8 2.2 copy-start.3
  206.8 132.5 %copy-start.4 = (f32[32]{0:T(128)S(1)}, f32[32]{0:T(128)}, u32[]{:S(2)}) copy-start(f32[32]{0:T(128)} %param.8) | copy-start | bytes 388
  206.9 143.3 %copy-start.1 = (f32[8,8,128]{2,1,0:T(8,128)S(1)}, f32[8,8,128]{2,1,0:T(8,128)}, u32[]{:S(2)}) copy-start(f32[8,8,128]{2,1,0:T(8,128)} %param.7) | copy-start | bytes 98308
  331.7 16.3 %all-to-all-start.1 = ((f32[16,1,512]{2,1,0:T(1,128)}), f32[16,1,512]{2,1,0:T(1,128)S(1)}, u32[]{:S(2)}, u32[]{:S(2)}) async-start(f32[16,1,512]{2,1,0:T(1,128)} %reshape.130), calls=%async_computation.2 | async-start | bytes 65536 | tf_op jit(solution)/shard_map/all_to_all | solution.py:63
  339.3 205.4 %reduce-scatter.5.cloned.1.call-start = ((), (), s32[]{:S(2)}) async-start(), calls=%async_computation.7 | async-start | bytes 1081344 | tf_op jit(solution)/shard_map/reduce_scatter | solution.py:55
Sparse Core Ops, SparseCore 0:
  28.7 104.9 all-gather.1
  209.2 120.6 reduce-scatter.2
  423.9 120.7 reduce-scatter.4
